TPU v7x, 32 devices: a whole 2x2x4 slice. The times are simulated.
32 devices in a mesh: seq: 8 (over z, x), head: 4 (over y, core).
Axes of the slice: x: 2, y: 2, z: 4, core: 2. Of those that a mesh axis runs over, the one named last changes fastest.
Arguments:
- layer_input: bfloat16 [8192, 2048], P('seq', 'head'), may hold values from -6 to 6
- w_proj: bfloat16 [2048, 10240], P(None, 'head'), may hold values from -0.125 to 0.125
- w_beta: bfloat16 [2048, 32], P(None, 'head'), may hold values from -0.25 to 0.25
- beta_bias: float32 [32], P('head'), may hold values from -9 to 1
- d_out: bfloat16 [8192, 2048], P('seq', 'head'), may hold values from -6 to 6
Outputs:
- grad_input: bfloat16 [8192, 2048], P('seq', 'head')
- grad_proj: float32 [2048, 10240], P('seq', 'head')
- grad_beta: float32 [2048, 32], P('seq', 'head')
All inputs are finite; a program needn't handle non-finite values.
Results may differ from a plain program's by a relative error of at most 0.02.
Values may be sent and summed in bfloat16 or wider, within the bound.
No kernel may reach another device: no remote copies, remote signals or barrier semaphores. Data moves between devices by JAX's collectives and lax.ppermute only.
A program may use at most 192 MiB of HBM per device.

v0:
```python
import jax
import jax.numpy as jnp
from jax import lax
from jax.sharding import PartitionSpec as P

DK = 128
SPAN = 64


MAX_PRECISION = lax.Precision.HIGHEST


def from_behind(value, axis, by):
    devices = lax.axis_size(axis)
    pairs = [(i, i + by) for i in range(devices) if 0 <= i + by < devices]
    return lax.ppermute(value, axis, pairs)


def prepare(projected, logits):
    length = projected.shape[0]
    head_count = logits.shape[1] // 2
    blocks = length // SPAN
    sections = projected.reshape(length, head_count, 5, DK)
    queries = jnp.transpose(sections[:, :, 0], (1, 0, 2)).reshape(head_count, blocks, SPAN, DK)
    raw_keys = jnp.transpose(sections[:, :, 1:3], (1, 0, 2, 3)).reshape(
        head_count, blocks, 2 * SPAN, DK
    )
    values = jnp.transpose(sections[:, :, 3:5], (1, 0, 2, 3)).reshape(
        head_count, blocks, 2 * SPAN, DK
    )
    scaled_keys = raw_keys * lax.rsqrt(jnp.sum(raw_keys * raw_keys, axis=-1, keepdims=True) + 1e-06)
    strengths = 2.0 * jax.nn.sigmoid(
        jnp.transpose(logits.reshape(length, head_count, 2), (1, 0, 2)).reshape(
            head_count, blocks, 2 * SPAN
        )
    )
    intersections = jnp.einsum("hcik,hcjk->hcij", scaled_keys, scaled_keys, precision=MAX_PRECISION)
    lower_part = jnp.tril(strengths[..., :, None] * intersections, -1)
    system = lower_part + jnp.eye(2 * SPAN, dtype=jnp.float32)
    targets = strengths[..., None] * jnp.concatenate([scaled_keys, values], axis=-1)
    solved = jax.scipy.linalg.solve_triangular(system, targets, lower=True)
    return (queries, scaled_keys, solved[..., :DK], solved[..., DK:])


def visible_mask():
    read_index = jnp.arange(SPAN, dtype=jnp.int32)[:, None]
    writes = jnp.arange(2 * SPAN, dtype=jnp.int32)[None, :]
    return (writes <= 2 * read_index + 1).astype(jnp.float32)


def run_spans(queries, scaled_keys, weights_w, updates, initial):
    visible = visible_mask()

    def advance(carried_state, inputs):
        query_tile, key_tile, wide_tile, update_tile = inputs
        delta_rows = update_tile - jnp.einsum(
            "lyx,lxg->lyg", wide_tile, carried_state, precision=MAX_PRECISION
        )
        score_matrix = (
            jnp.einsum("hik,hjk->hij", query_tile, key_tile, precision=MAX_PRECISION) * visible
        )
        produced_output = jnp.einsum(
            "lyx,lxg->lyg", query_tile, carried_state, precision=MAX_PRECISION
        ) + jnp.einsum("sml,slo->smo", score_matrix, delta_rows, precision=MAX_PRECISION)
        carried_state = carried_state + jnp.einsum(
            "qnz,qna->qza", key_tile, delta_rows, precision=MAX_PRECISION
        )
        return (carried_state, produced_output)

    stacked = tuple(
        (jnp.moveaxis(member, 1, 0) for member in (queries, scaled_keys, weights_w, updates))
    )
    final_state, produced_output = lax.scan(advance, initial, stacked)
    head_count = initial.shape[0]
    outputs = jnp.transpose(produced_output, (0, 2, 1, 3)).reshape(-1, head_count * DK)
    return (outputs, final_state)


def combine_maps(earlier, later):
    first_map, first_shift = earlier
    second_map, second_shift = later
    joined = jnp.einsum("hij,hjk->hik", second_map, first_map, precision=MAX_PRECISION)
    shifted = (
        jnp.einsum("hij,hjk->hik", second_map, first_shift, precision=MAX_PRECISION) + second_shift
    )
    return (joined, shifted)


def shards(layer_input, w_proj, w_beta, beta_bias, d_out):
    whole = lax.all_gather(layer_input, "head", axis=1, tiled=True)
    projected = jnp.dot(whole, w_proj, preferred_element_type=jnp.float32).astype(jnp.bfloat16)
    logits = jnp.dot(whole, w_beta, preferred_element_type=jnp.float32) + beta_bias
    stored = lax.optimization_barrier(projected)
    prepared, pull_prepare = jax.vjp(prepare, stored.astype(jnp.float32), logits)
    queries, scaled_keys, weights_w, updates = prepared
    head_count = queries.shape[0]
    blocks = queries.shape[1]
    identity = jnp.broadcast_to(jnp.eye(DK, dtype=jnp.float32), (head_count, DK, DK))
    zero_state = jnp.zeros((head_count, DK, DK), jnp.float32)
    transitions = identity[:, None] - jnp.einsum(
        "hcjk,hcjl->hckl", scaled_keys, weights_w, precision=MAX_PRECISION
    )
    offsets = jnp.einsum("hcjk,hcjv->hckv", scaled_keys, updates, precision=MAX_PRECISION)

    def forward_fold(carried_state, block_pair):
        return (combine_maps(carried_state, block_pair), None)

    (shard_transition, shard_offset), unused_one = lax.scan(
        forward_fold,
        (identity, zero_state),
        (jnp.moveaxis(transitions, 1, 0), jnp.moveaxis(offsets, 1, 0)),
    )
    cotangent = d_out.astype(jnp.float32)
    blocked_grad = jnp.transpose(cotangent.reshape(blocks, SPAN, head_count, DK), (2, 0, 1, 3))
    score_matrix = (
        jnp.einsum("hcik,hcjk->hcij", queries, scaled_keys, precision=MAX_PRECISION)
        * visible_mask()
    )
    readout = queries - jnp.einsum(
        "hcij,hcjk->hcik", score_matrix, weights_w, precision=MAX_PRECISION
    )
    sources = jnp.einsum("hcik,hciv->hckv", readout, blocked_grad, precision=MAX_PRECISION)

    def backward_fold(carried_state, block_pair):
        transition, source = block_pair
        return (
            jnp.einsum("hji,hjk->hik", transition, carried_state, precision=MAX_PRECISION) + source,
            None,
        )

    shard_source, unused_two = lax.scan(
        backward_fold,
        zero_state,
        (jnp.moveaxis(transitions, 1, 0), jnp.moveaxis(sources, 1, 0)),
        reverse=True,
    )
    transposed = jnp.swapaxes(shard_transition, 1, 2)

    def hop(index, carried_state):
        start_state, end_grad = carried_state
        leaving = (
            jnp.einsum("hij,hjk->hik", shard_transition, start_state, precision=MAX_PRECISION)
            + shard_offset
        )
        arriving = (
            jnp.einsum("hij,hjk->hik", transposed, end_grad, precision=MAX_PRECISION) + shard_source
        )
        start_state = from_behind(leaving.astype(jnp.bfloat16), "seq", 1).astype(leaving.dtype)
        end_grad = from_behind(arriving.astype(jnp.bfloat16), "seq", -1).astype(arriving.dtype)
        return (start_state, end_grad)

    start_state, end_grad = lax.fori_loop(
        0, lax.axis_size("seq") - 1, hop, (zero_state, zero_state)
    )
    (outputs, final_state), pull_run = jax.vjp(
        run_spans, queries, scaled_keys, weights_w, updates, start_state
    )
    pulled = pull_run((cotangent, end_grad))
    grad_projected, grad_logits = pull_prepare(pulled[:4])
    grad_projected = grad_projected.astype(jnp.bfloat16)
    grad_logits = grad_logits.astype(jnp.bfloat16)
    partial_input = jnp.einsum(
        "tc,dc->td", grad_projected, w_proj, preferred_element_type=jnp.float32
    ) + jnp.einsum("tc,dc->td", grad_logits, w_beta, preferred_element_type=jnp.float32)
    grad_input = lax.psum_scatter(
        partial_input.astype(jnp.bfloat16), "head", scatter_dimension=1, tiled=True
    )
    grad_weights = jnp.einsum(
        "td,tc->dc", whole, grad_projected, preferred_element_type=jnp.float32
    )
    grad_rates = jnp.einsum("td,tc->dc", whole, grad_logits, preferred_element_type=jnp.float32)
    grad_proj, grad_beta = (
        lax.psum_scatter(
            grad_weights.astype(jnp.bfloat16), "seq", scatter_dimension=0, tiled=True
        ).astype(jnp.float32),
        lax.psum_scatter(
            grad_rates.astype(jnp.bfloat16), "seq", scatter_dimension=0, tiled=True
        ).astype(jnp.float32),
    )
    return (grad_input, grad_proj, grad_beta)


def solution(mesh):
    in_specs = (P("seq", "head"), P(None, "head"), P(None, "head"), P("head"), P("seq", "head"))
    out_specs = (P("seq", "head"), P("seq", "head"), P("seq", "head"))
    return jax.shard_map(shards, mesh=mesh, in_specs=in_specs, out_specs=out_specs, check_vma=False)
```

profile of v0, /device:TPU:0, one launch (start us, length us, event | category | flops | bytes accessed | tf_op | source)
XLA Modules:
  0.0 1775.7 jit_solution(2887152884586890000)
XLA Ops:
  11.1 35.7 %all-gather.2.cloned.1.call-done = bf16[1024,2048]{1,0:T(8,128)(2,1)} async-done(((bf16[1024,512]{1,0:T(8,128)(2,1)}), bf16[1024,2048]{1,0:T(8,128)(2,1)}) %all-gather.2.cloned.1.call-update) | async-done | bytes 4194320 | tf_op jit(solution)/shard_map/all_gather | solution.py:90
  46.8 16.5 convolution_convert_fusion.1
  63.3 7.9 copy.167
  71.2 3.8 reshape.176
  75.0 4.2 slice_bitcast_fusion
  83.5 7.2 copy.168
  91.7 2.9 broadcast_multiply_fusion.1
  94.6 10.5 fusion.141
  109.9 4.2 select_bitcast_fusion
  114.1 630.2 %custom-call.10 = f32[4,16,1,128,128]{3,4,2,1,0:T(8,128)} custom-call(f32[4,16,1,128,128]{4,3,2,1,0:T(8,128)} %select_bitcast_fusion), custom_call_target="InvertDiagBlocksLowerTriangular" | custom-call | tf_op jit(solution)/shard_map/jvp(jit(_solve_triangular))/vmap(vmap())/triangular_solve | solution.py:41
  744.3 7.2 copy.173
  751.6 13.1 fusion.86
  764.7 8.7 subtract_bitcast_fusion
  773.4 8.5 fusion.110
  781.9 4.4 slice_bitcast_fusion.2
  787.9 7.7 fusion.142
  795.6 2.9 copy.180
  798.5 6.2 fusion.105
  804.8 5.1 convolution_bitcast_fusion.1
  809.8 27.1 %while.84 = (s32[]{:T(128)}, f32[4,128,128]{2,1,0:T(8,128)S(1)}, f32[16,4,128,128]{3,2,0,1:T(8,128)}, f32[16,4,128,128]{3,2,0,1:T(8,128)}, s32[]{:T(128)}, /*index=5*/s32[]{:T(128)}, s32[]{:T(128)}) while((s32[]{:T(128)}, f32[4,128,128]{2,1,0:T(8,128)S(1)}, f32[16,4,128,128]{3,2,0,1:T(8,128)}, f32[16,4,128,128]{3,2,0,1:T(8,128)}, ...), condition=%wide.region_4.5_spmd.clone, body=%wide.region_3.4_spmd.clone.sunk | while | flops 100794368 | bytes 1574498 | solution.py:131
  836.9 45.9 %while.83 = (s32[]{:T(128)}, f32[4,128,128]{2,1,0:T(8,128)S(1)}, f32[4,128,128]{2,1,0:T(8,128)S(1)}, f32[16,4,128,128]{3,2,0,1:T(8,128)}, f32[16,4,128,128]{3,2,0,1:T(8,128)}, /*index=5*/s32[]{:T(128)}, s32[]{:T(128)}) while((s32[]{:T(128)}, f32[4,128,128]{2,1,0:T(8,128)S(1)}, f32[4,128,128]{2,1,0:T(8,128)S(1)}, ...), condition=%wide.region_2.3_spmd.clone, body=%wide.region_1.2_spmd.clone.sunk | while | flops 201457664 | bytes 2885207 | solution.py:108
  882.9 4.3 fusion.175
  888.7 80.9 %while.85 = (s32[]{:T(128)}, f32[4,128,128]{2,1,0:T(8,128)S(1)}, f32[4,128,128]{2,1,0:T(8,128)S(1)}, f32[4,128,128]{2,1,0:T(8,128)S(1)}, f32[4,128,128]{2,1,0:T(...) while((s32[]{:T(128)}, f32[4,128,128]{2,1,0:T(8,128)S(1)}, ...), condition=%wide.region_6.7_spmd.clone, body=%wide.region_5.6_spmd.clone.sunk | while | flops 201850880 | bytes 3670200 | solution.py:152
  889.1 3.4 collective-permute-start
  895.6 4.5 collective-permute-done.1
  900.6 4.3 collective-permute-start
  907.4 4.7 collective-permute-done.1
  912.6 3.6 collective-permute-start
  920.1 3.3 collective-permute-done.1
  923.9 4.1 collective-permute-start
  931.8 3.4 collective-permute-done.1
  935.6 3.6 collective-permute-start
  943.1 3.4 collective-permute-done.1
  946.9 4.1 collective-permute-start
  954.9 3.4 collective-permute-done.1
  958.7 3.6 collective-permute-start
  966.2 3.4 collective-permute-done.1
  969.6 2.5 broadcast.173.clone.2
  972.1 2.6 broadcast.173.clone.3
  974.7 108.4 %while.81 = (s32[]{:T(128)}, f32[4,128,128]{2,1,0:T(8,128)S(1)}, f32[16,4,128,128]{3,2,1,0:T(8,128)}, f32[16,4,128,128]{3,2,1,0:T(8,128)}, f32[16,4,64,128]{3,2,...) while((s32[]{:T(128)}, f32[4,128,128]{2,1,0:T(8,128)S(1)}, ...), condition=%wide.region_8.9_spmd.clone, body=%wide.region_7.8_spmd.clone.sunk | while | flops 251838464 | bytes 3477357 | solution.py:73
  1083.1 2.5 broadcast.173
  1085.6 2.5 broadcast.173.clone
  1088.1 2.5 broadcast.173.clone.1
  1092.1 302.5 %while.82 = (s32[]{:T(128)}, f32[4,128,128]{2,1,0:T(8,128)S(1)}, f32[16,4,64,128]{3,2,0,1:T(8,128)}, f32[16,4,128,128]{3,2,0,1:T(8,128)}, f32[16,4,128,128]{3,2,...) while((s32[]{:T(128)}, f32[4,128,128]{2,1,0:T(8,128)S(1)}, ...), condition=%wide.region_10.11_spmd.clone, body=%wide.region_9.10_spmd.clone.sunk | while | flops 705118208 | bytes 8065469 | solution.py:73
  1191.2 2.3 fusion.242
  1229.0 2.3 fusion.242
  1342.4 2.3 fusion.242
  1394.6 14.8 multiply_reduce_fusion
  1409.3 12.7 fusion.88
  1422.1 15.7 multiply_reduce_fusion.1
  1439.4 10.5 fusion.101
  1449.8 2.6 split.8
  1454.6 13.3 multiply_reduce_fusion.2
  1467.8 4.4 add_add_fusion
  1472.8 4.5 add_convert_fusion
  1477.3 8.1 copy.204
  1485.4 3.5 fusion.109
  1489.0 16.6 fusion.85
  1505.6 15.4 fusion.143
  1521.0 3.4 add_convert_fusion.1
  1524.5 16.6 reduce-scatter.8.cloned.1.call-done
  1542.3 179.9 %reduce-scatter.6.cloned.1.call-done = bf16[256,2560]{0,1:T(8,128)(2,1)} async-done(((bf16[2048,2560]{0,1:T(8,128)(2,1)}), bf16[256,2560]{0,1:T(8,128)(2,1)}) %reduce-scatter.6.cloned.1.call-update) | async-done | bytes 1310736 | tf_op jit(solution)/shard_map/reduce_scatter | solution.py:173
  1722.2 2.8 copy.208
  1725.0 43.8 %reduce-scatter.4.cloned.1.call-done = bf16[1024,512]{1,0:T(8,128)(2,1)} async-done(((bf16[1024,2048]{1,0:T(8,128)(2,1)}), bf16[1024,512]{1,0:T(8,128)(2,1)}) %reduce-scatter.4.cloned.1.call-update) | async-done | bytes 1048592 | tf_op jit(solution)/shard_map/reduce_scatter | solution.py:165
  (487 shorter events, 526.7 us)
Async XLA Ops:
  7.2 97.9 %copy-start = (bf16[2048,8]{0,1:T(8,128)(2,1)S(1)}, bf16[2048,8]{0,1:T(8,128)(2,1)}, u32[]{:S(2)}) copy-start(bf16[2048,8]{0,1:T(8,128)(2,1)} %param.17) | copy-start | bytes 98308
  7.2 39.6 %all-gather.2.cloned.1.call-start = ((), (), s32[]{:S(2)}) async-start(), calls=%async_computation.3 | async-start | bytes 5242880 | tf_op jit(solution)/shard_map/all_gather | solution.py:90
  7.9 1533.1 %reduce-scatter.8.cloned.1.call-start = ((), (), s32[]{:S(2)}) async-start(), calls=%async_computation.6 | async-start | bytes 36864 | tf_op jit(solution)/shard_map/reduce_scatter | solution.py:176
  9.4 53.9 %copy-start.12 = (bf16[16,64,4,128]{3,2,1,0:T(4,128)(2,1)}, bf16[16,64,4,128]{3,2,1,0:T(4,128)(2,1)S(1)}, u32[]{:S(2)}) copy-start(bf16[16,64,4,128]{3,2,1,0:T(4,128)(2,1)S(1)} %reshape.181) | copy-start | bytes 3145732
  94.5 10.5 copy-start.1
  94.6 10.6 copy-start.9
  94.6 10.6 copy-start.16
  106.9 7.2 copy-start.14
  751.6 13.1 copy-start.2
  764.7 17.2 copy-start.4
  798.5 6.2 copy-start.10
  798.5 6.3 copy-start.13
  882.9 4.3 copy-start.11
  889.1 6.5 collective-permute-start
  892.9 7.3 collective-permute-start.1
  900.6 6.8 collective-permute-start
  905.3 6.9 collective-permute-start.1
  912.6 7.5 collective-permute-start
  916.6 6.9 collective-permute-start.1
  923.9 7.9 collective-permute-start
  928.3 6.9 collective-permute-start.1
  935.6 7.5 collective-permute-start
  939.6 6.9 collective-permute-start.1
  946.9 8.0 collective-permute-start
  951.4 6.9 collective-permute-start.1
  958.7 7.4 collective-permute-start
  962.7 6.9 collective-permute-start.1
  1394.6 14.8 copy-start.6
  1394.6 14.8 copy-start.7
  1422.0 16.0 copy-start.15
  1439.3 13.1 copy-start.8
  1449.8 3.4 copy-start.3
  1449.8 4.7 copy-start.5
  1488.9 233.3 %reduce-scatter.6.cloned.1.call-start = ((), (), s32[]{:S(2)}) async-start(), calls=%async_computation.5 | async-start | bytes 11796480 | tf_op jit(solution)/shard_map/reduce_scatter | solution.py:173
  1505.6 263.2 %reduce-scatter.4.cloned.1.call-start = ((), (), s32[]{:S(2)}) async-start(), calls=%async_computation.4 | async-start | bytes 5242880 | tf_op jit(solution)/shard_map/reduce_scatter | solution.py:165
Sparse Core Ops, SparseCore 0:
  9.6 37.1 all-gather.1
  1489.0 51.9 reduce-scatter.7
  1544.6 177.5 reduce-scatter.5
  1725.2 43.5 reduce-scatter.3
where the time goes:
time: 1790 us; the launch traced here: 1780 us
  other arithmetic  662 us (37%)
  matrix products  641 us (36%)
  waiting for transfers between devices  316 us (18%)
  local copies, waits for them, and re-layouts  104 us (6%)
  starting transfers between devices  35.8 us (2%)
    another operation x2, other arithmetic, prepare(): solved = jax.scipy.linalg.solve_triangular(system, targets, lower=True)  634 us
    reduce_scatter x1, waiting for transfers between devices, shards(): lax.psum_scatter(grad_weights.astype(jnp.bfloat16), 'seq', scatter_dimens...  180 us
    dot_general x48, matrix products, advance(): jnp.einsum('hik,hjk->hij', query_tile, key_tile, precision=MAX_PRECISION)  104 us
    dot_general x48, matrix products, advance(): jnp.einsum('lyx,lxg->lyg', wide_tile, carried_state, precision=MAX_PRECIS...  95.9 us
    dot_general x48, matrix products, advance(): jnp.einsum('qnz,qna->qza', key_tile, delta_rows, precision=MAX_PRECISION)  72.3 us
    dot_general x32, matrix products, advance(): jnp.einsum('sml,slo->smo', score_matrix, delta_rows, precision=MAX_PRECIS...  60.4 us
    dot_general x32, matrix products, advance(): jnp.einsum('lyx,lxg->lyg', query_tile, carried_state, precision=MAX_PRECI...  48.9 us
    reduce_scatter x1, waiting for transfers between devices, shards(): lax.psum_scatter(partial_input.astype(jnp.bfloat16), 'head', scatter_dime...  43.8 us
  transfers between devices with their start and end apart: 18, of which 18 were waited for; matrix products, arithmetic and copies ran while one was open for 3% of the time, Pallas kernels for 0%

commit v1 on v0

v1 whole, which is shorter than its diff:
```python
import functools

import jax
import jax.numpy as jnp
import numpy as np
from jax import lax
from jax.experimental import pallas as pl
from jax.experimental.pallas import tpu as pltpu
from jax.sharding import PartitionSpec as P

DK = 128
SPAN = 64
ROWS = 2 * SPAN
BASE = 16
HALF = BASE // 2
COLS = 5 * DK
BF = jnp.bfloat16
F32 = jnp.float32
VMEM_LIMIT = 56 << 20


def dot(a, b, ca, cb):
    return lax.dot_general(
        a.astype(BF), b.astype(BF), (((ca,), (cb,)), ((), ())), preferred_element_type=F32
    )


def nn(a, b):
    return dot(a, b, 1, 0)


def nt(a, b):
    return dot(a, b, 1, 1)


def tn(a, b):
    return dot(a, b, 0, 0)


def split(a):
    high = a.astype(BF)
    return high, (a - high.astype(F32)).astype(BF)


def nn3(a, b):
    ah, al = split(a)
    bh, bl = split(b)
    return nn(jnp.concatenate([ah, al], 1), jnp.concatenate([bh, bh], 0)) + nn(ah, bl)


def nt3(a, b):
    ah, al = split(a)
    bh, bl = split(b)
    return nt(jnp.concatenate([ah, al], 1), jnp.concatenate([bh, bh], 1)) + nt(ah, bl)


def rows_cols(rows, cols):
    row = lax.broadcasted_iota(jnp.int32, (rows, cols), 0)
    col = lax.broadcasted_iota(jnp.int32, (rows, cols), 1)
    return row, col


def order(index):
    return 2 * (index % SPAN) + index // SPAN


def strict_mask():
    row, col = rows_cols(ROWS, ROWS)
    return order(col) < order(row)


def visible_mask():
    row, col = rows_cols(SPAN, ROWS)
    return col % SPAN <= row


def stack_steps(ref, rows, first):
    return jnp.concatenate(
        [ref[rows, first * DK : (first + 1) * DK], ref[rows, (first + 1) * DK : (first + 2) * DK]], 0
    ).astype(F32)


def strengths_of(logit_ref, rows):
    pair = logit_ref[0, rows, :]
    return 2.0 * jax.nn.sigmoid(jnp.concatenate([pair[:, 0:1], pair[:, 1:2]], 0))


def spread_table():
    table = np.zeros((DK, BASE, DK), np.float32)
    for lane in range(DK):
        group = (lane % SPAN) // HALF
        for member in range(BASE):
            source = (member // HALF) * SPAN + group * HALF + member % HALF
            table[source, member, lane] = 1.0
    return table.reshape(DK, BASE * DK)


def local_kernel(
    blocks,
    unroll,
    spread_ref,
    proj_ref,
    logit_ref,
    grad_ref,
    key_ref,
    inv_ref,
    wide_ref,
    upd_ref,
    read_ref,
    map_ref,
    shift_ref,
    source_ref,
    total_ref,
    system,
    packed,
    coef,
    solved,
    maps,
    shifts,
    sources,
):
    strict = strict_mask()
    lane_group = (rows_cols(HALF, ROWS)[1] % SPAN) // HALF

    def first(outer, carry):
        for inner in range(unroll):
            block = outer * unroll + inner
            rows = pl.ds(pl.multiple_of(block * SPAN, SPAN), SPAN)
            raw = stack_steps(proj_ref, rows, 1)
            strengths = strengths_of(logit_ref, rows)
            keys = raw * lax.rsqrt(jnp.sum(raw * raw, axis=1, keepdims=True) + 1e-06)
            key_ref[0, block] = keys.astype(BF)
            lower = jnp.where(strict, strengths * nt3(keys, keys), 0.0)
            system[block] = lower
            for step in range(2):
                piece = jnp.zeros((HALF, ROWS), F32)
                for group in range(SPAN // HALF):
                    start = step * SPAN + group * HALF
                    piece = jnp.where(lane_group == group, lower[start : start + HALF], piece)
                packed[pl.ds(step * HALF * blocks + block, HALF, stride=blocks), :] = piece
        return carry

    lax.fori_loop(0, blocks // unroll, first, 0)

    high, low = split(packed[...])
    spread = spread_ref[...]
    coef[...] = nn(jnp.concatenate([high, low], 1), jnp.concatenate([spread, spread], 0))
    lane = rows_cols(blocks, ROWS)[1]
    found = {}
    for when in range(BASE):
        step, tick = when % 2, when // 2
        here = step * HALF + tick
        value = jnp.where((lane // SPAN == step) & (lane % HALF == tick), 1.0, 0.0)
        for before in range(when):
            there = (before % 2) * HALF + before // 2
            weight = coef[here * blocks : (here + 1) * blocks, there * ROWS : (there + 1) * ROWS]
            value = value - weight * found[before]
        found[when] = value
        solved[here * blocks : (here + 1) * blocks, :] = value

    row, col = rows_cols(ROWS, ROWS)
    row_time, col_time = order(row), order(col)
    visible = visible_mask()

    def second(outer, carry):
        for inner in range(unroll):
            block = outer * unroll + inner
            rows = pl.ds(pl.multiple_of(block * SPAN, SPAN), SPAN)
            pieces = []
            for step in range(2):
                piece = solved[pl.ds(step * HALF * blocks + block, HALF, stride=blocks), :]
                for group in range(SPAN // HALF):
                    pieces.append(jnp.where(lane_group == group, piece, 0.0))
            inverse = jnp.concatenate(pieces, 0)
            lower = system[block]
            size = BASE
            while size < ROWS:
                joins = (row_time // (2 * size) == col_time // (2 * size)) & (
                    row_time // size != col_time // size
                )
                inverse = inverse - nn3(inverse, nn3(jnp.where(joins, lower, 0.0), inverse))
                size *= 2
            strengths = strengths_of(logit_ref, rows)
            keys = key_ref[0, block]
            values = stack_steps(proj_ref, rows, 3)
            query = proj_ref[rows, 0:DK]
            cotangent = grad_ref[rows, :]
            inverse_bf = inverse.astype(BF)
            inv_ref[0, block] = inverse_bf
            targets = jnp.concatenate([strengths * keys.astype(F32), strengths * values], 1)
            both = nn(inverse_bf, targets)
            both_bf = both.astype(BF)
            wide_bf = both_bf[:, :DK]
            wide_ref[0, block] = wide_bf
            upd_ref[0, block] = both_bf[:, DK:]
            score = jnp.where(visible, nt(query, keys), 0.0)
            reads = tn(score, cotangent)
            read_ref[0, block] = reads.astype(BF)
            folded = tn(keys, both_bf)
            maps[block] = -folded[:, :DK]
            shifts[block] = folded[:, DK:]
            sources[block] = tn(query, cotangent) - tn(wide_bf, reads)
        return carry

    lax.fori_loop(0, blocks // unroll, second, 0)

    offset, count = 0, blocks
    while count > 1:
        for pair in range(count // 2):
            left, right, parent = offset + 2 * pair, offset + 2 * pair + 1, offset + count + pair
            near, far = maps[left], maps[right]
            joined = nn(far, jnp.concatenate([near, shifts[left]], 1))
            maps[parent] = near + far + joined[:, :DK]
            shifts[parent] = shifts[left] + shifts[right] + joined[:, DK:]
            later = sources[right]
            sources[parent] = sources[left] + later + tn(near, later)
        offset += count
        count //= 2
    map_ref[0] = maps[...].astype(BF)
    shift_ref[0] = shifts[...].astype(BF)
    source_ref[0] = sources[...].astype(BF)
    total_ref[0, 0] = maps[offset]
    total_ref[0, 1] = shifts[offset]
    total_ref[0, 2] = sources[offset]


def params():
    return pltpu.CompilerParams(
        dimension_semantics=("arbitrary",), vmem_limit_bytes=VMEM_LIMIT
    )


def local_pass(projected, logits, d_out, first_head, heads):
    tokens = projected.shape[0]
    blocks = tokens // SPAN
    nodes = 2 * blocks - 1
    square = jax.ShapeDtypeStruct((heads, blocks, ROWS, DK), BF)
    tree = jax.ShapeDtypeStruct((heads, nodes, DK, DK), BF)
    tile = pl.BlockSpec((1, blocks, ROWS, DK), lambda h: (h, 0, 0, 0))
    branch = pl.BlockSpec((1, nodes, DK, DK), lambda h: (h, 0, 0, 0))
    unroll = 2
    return pl.pallas_call(
        functools.partial(local_kernel, blocks, unroll),
        grid=(heads,),
        out_shape=(square,) * 5
        + (tree,) * 3
        + (jax.ShapeDtypeStruct((heads, 3, DK, DK), F32),),
        in_specs=[
            pl.BlockSpec((DK, BASE * DK), lambda h: (0, 0)),
            pl.BlockSpec((tokens, COLS), lambda h: (0, first_head + h)),
            pl.BlockSpec((1, tokens, 2), lambda h: (first_head + h, 0, 0)),
            pl.BlockSpec((tokens, DK), lambda h: (0, first_head + h)),
        ],
        out_specs=(tile,) * 5
        + (branch,) * 3
        + (pl.BlockSpec((1, 3, DK, DK), lambda h: (h, 0, 0, 0)),),
        scratch_shapes=[
            pltpu.VMEM((blocks, ROWS, ROWS), F32),
            pltpu.VMEM((BASE * blocks, ROWS), F32),
            pltpu.VMEM((BASE * blocks, BASE * ROWS), F32),
            pltpu.VMEM((BASE * blocks, ROWS), F32),
            pltpu.VMEM((nodes, DK, DK), F32),
            pltpu.VMEM((nodes, DK, DK), F32),
            pltpu.VMEM((nodes, DK, DK), F32),
        ],
        compiler_params=params(),
        cost_estimate=pl.CostEstimate(
            flops=heads * blocks * 60 * DK**3, bytes_accessed=heads * 8 << 20, transcendentals=0
        ),
        name="local_pass",
    )(jnp.asarray(spread_table(), BF), projected, logits, d_out)


def grad_kernel(
    blocks,
    unroll,
    proj_ref,
    logit_ref,
    grad_ref,
    key_ref,
    inv_ref,
    wide_ref,
    upd_ref,
    read_ref,
    map_ref,
    shift_ref,
    source_ref,
    edge_ref,
    out_ref,
    rate_ref,
    states,
    ends,
):
    nodes = 2 * blocks - 1
    states[nodes - 1] = edge_ref[0, 0]
    ends[nodes - 1] = edge_ref[0, 1]
    count, offset = 2, nodes - 3
    while count <= blocks:
        for pair in range(count // 2):
            left, right, parent = offset + 2 * pair, offset + 2 * pair + 1, offset + count + pair
            state, end = states[parent], ends[parent]
            states[left] = state
            states[right] = state + nn(map_ref[0, left], state) + shift_ref[0, left].astype(F32)
            ends[right] = end
            ends[left] = end + tn(map_ref[0, right], end) + source_ref[0, right].astype(F32)
        count *= 2
        offset -= count

    strict = strict_mask()
    visible = visible_mask()

    def body(outer, carry):
        for inner in range(unroll):
            block = outer * unroll + inner
            rows = pl.ds(pl.multiple_of(block * SPAN, SPAN), SPAN)
            raw = stack_steps(proj_ref, rows, 1)
            scale = lax.rsqrt(jnp.sum(raw * raw, axis=1, keepdims=True) + 1e-06)
            keys = raw * scale
            keys_bf = key_ref[0, block]
            strengths = strengths_of(logit_ref, rows)
            values = stack_steps(proj_ref, rows, 3)
            query = proj_ref[rows, 0:DK]
            cotangent = grad_ref[rows, :]
            state = states[block].astype(BF)
            end = ends[block].astype(BF)
            delta = (upd_ref[0, block].astype(F32) - nn(wide_ref[0, block], state)).astype(BF)
            back = read_ref[0, block].astype(F32) + nn(keys_bf, end)
            held = tn(inv_ref[0, block], back)
            many = nt(
                jnp.concatenate([cotangent, held.astype(BF)], 0),
                jnp.concatenate([delta, state], 0),
            )
            seen = jnp.where(visible, many[:SPAN, :ROWS], 0.0).astype(BF)
            crossed = jnp.where(strict, many[SPAN:, :ROWS], 0.0).astype(BF)
            onward = nn(jnp.concatenate([seen, crossed], 0), keys_bf)
            d_query = many[:SPAN, ROWS:] + onward[:SPAN]
            inner_sum = many[SPAN:, ROWS:] + onward[SPAN:]
            d_keys = (
                tn(
                    jnp.concatenate([seen, crossed], 0),
                    jnp.concatenate([query, (-strengths * keys).astype(BF)], 0),
                )
                + nt(delta, end)
                - strengths * inner_sum
            )
            d_values = strengths * held
            d_rate = jnp.sum(held * values - keys * inner_sum, axis=1, keepdims=True)
            d_raw = scale * (d_keys - keys * jnp.sum(keys * d_keys, axis=1, keepdims=True))
            d_logit = d_rate * strengths * (1.0 - 0.5 * strengths)
            out_ref[rows, 0:DK] = d_query.astype(BF)
            out_ref[rows, DK : 2 * DK] = d_raw[:SPAN].astype(BF)
            out_ref[rows, 2 * DK : 3 * DK] = d_raw[SPAN:].astype(BF)
            out_ref[rows, 3 * DK : 4 * DK] = d_values[:SPAN].astype(BF)
            out_ref[rows, 4 * DK : 5 * DK] = d_values[SPAN:].astype(BF)
            rate_ref[0, rows, :] = jnp.concatenate([d_logit[:SPAN], d_logit[SPAN:]], 1)
        return carry

    lax.fori_loop(0, blocks // unroll, body, 0)


def grad_pass(projected, logits, d_out, kept, edges, first_head, heads):
    tokens = projected.shape[0]
    blocks = tokens // SPAN
    nodes = 2 * blocks - 1
    tile = pl.BlockSpec((1, blocks, ROWS, DK), lambda h: (h, 0, 0, 0))
    branch = pl.BlockSpec((1, nodes, DK, DK), lambda h: (h, 0, 0, 0))
    unroll = 2
    return pl.pallas_call(
        functools.partial(grad_kernel, blocks, unroll),
        grid=(heads,),
        out_shape=(
            jax.ShapeDtypeStruct((tokens, heads * COLS), BF),
            jax.ShapeDtypeStruct((heads, tokens, 2), F32),
        ),
        in_specs=[
            pl.BlockSpec((tokens, COLS), lambda h: (0, first_head + h)),
            pl.BlockSpec((1, tokens, 2), lambda h: (first_head + h, 0, 0)),
            pl.BlockSpec((tokens, DK), lambda h: (0, first_head + h)),
        ]
        + [tile] * 5
        + [branch] * 3
        + [pl.BlockSpec((1, 2, DK, DK), lambda h: (h, 0, 0, 0))],
        out_specs=(
            pl.BlockSpec((tokens, COLS), lambda h: (0, h)),
            pl.BlockSpec((1, tokens, 2), lambda h: (h, 0, 0)),
        ),
        scratch_shapes=[
            pltpu.VMEM((nodes, DK, DK), F32),
            pltpu.VMEM((nodes, DK, DK), F32),
        ],
        compiler_params=params(),
        cost_estimate=pl.CostEstimate(
            flops=heads * blocks * 30 * DK**3, bytes_accessed=heads * 8 << 20, transcendentals=0
        ),
        name="grad_pass",
    )(projected, logits, d_out, *kept, edges)


def bmm(a, b):
    return jnp.einsum("hij,hjk->hik", a.astype(BF), b.astype(BF), preferred_element_type=F32)


def bmm_t(a, b):
    return jnp.einsum("hji,hjk->hik", a.astype(BF), b.astype(BF), preferred_element_type=F32)


def shifted(value, by):
    devices = lax.axis_size("seq")
    pairs = [(i, i + by) for i in range(devices) if 0 <= i + by < devices]
    return lax.ppermute(value.astype(BF), "seq", pairs).astype(F32)


def exchange(total):
    devices = lax.axis_size("seq")
    tail_map, tail_shift, head_source = total[:, 0], total[:, 1], total[:, 2]
    head_map = tail_map
    past_map = past_shift = next_map = next_source = None
    by = 1
    while by < devices:
        last = 2 * by >= devices
        if last:
            got_shift = shifted(tail_shift, by)
            got_source = shifted(head_source, -by)
        else:
            behind = shifted(jnp.concatenate([tail_map, tail_shift], 2), by)
            ahead = shifted(jnp.concatenate([head_map, head_source], 2), -by)
            got_map, got_shift = behind[:, :, :DK], behind[:, :, DK:]
            got_next, got_source = ahead[:, :, :DK], ahead[:, :, DK:]
        if past_map is None:
            past_shift, next_source = got_shift, got_source
        else:
            past_shift = past_shift + got_shift + bmm(past_map, got_shift)
            next_source = next_source + got_source + bmm_t(next_map, got_source)
        if not last:
            if past_map is None:
                past_map, next_map = got_map, got_next
            else:
                past_map = past_map + got_map + bmm(past_map, got_map)
                next_map = next_map + got_next + bmm(got_next, next_map)
            tail_shift = tail_shift + got_shift + bmm(tail_map, got_shift)
            head_source = head_source + got_source + bmm_t(head_map, got_source)
            tail_map = tail_map + got_map + bmm(tail_map, got_map)
            head_map = head_map + got_next + bmm(got_next, head_map)
        by *= 2
    return jnp.stack([past_shift, next_source], 1)


def shards(layer_input, w_proj, w_beta, beta_bias, d_out):
    whole = lax.all_gather(layer_input, "head", axis=1, tiled=True)
    tokens = whole.shape[0]
    heads = w_beta.shape[1] // 2
    projected = jnp.dot(whole, w_proj, preferred_element_type=F32).astype(BF)
    logits = jnp.dot(whole, w_beta, preferred_element_type=F32) + beta_bias
    logits = jnp.transpose(logits.reshape(tokens, heads, 2), (1, 0, 2))
    *kept, total = local_pass(projected, logits, d_out, 0, heads)
    edges = exchange(total)
    grad_projected, grad_logits = grad_pass(projected, logits, d_out, kept, edges, 0, heads)
    grad_logits = jnp.transpose(grad_logits, (1, 0, 2)).reshape(tokens, 2 * heads).astype(BF)
    partial_input = jnp.einsum(
        "tc,dc->td", grad_projected, w_proj, preferred_element_type=F32
    ) + jnp.einsum("tc,dc->td", grad_logits, w_beta, preferred_element_type=F32)
    grad_input = lax.psum_scatter(
        partial_input.astype(BF), "head", scatter_dimension=1, tiled=True
    )
    grad_weights = jnp.einsum("td,tc->dc", whole, grad_projected, preferred_element_type=F32)
    grad_rates = jnp.einsum("td,tc->dc", whole, grad_logits, preferred_element_type=F32)
    grad_proj = lax.psum_scatter(grad_weights.astype(BF), "seq", scatter_dimension=0, tiled=True)
    grad_beta = lax.psum_scatter(grad_rates.astype(BF), "seq", scatter_dimension=0, tiled=True)
    return (grad_input, grad_proj.astype(F32), grad_beta.astype(F32))


def solution(mesh):
    in_specs = (P("seq", "head"), P(None, "head"), P(None, "head"), P("head"), P("seq", "head"))
    out_specs = (P("seq", "head"), P("seq", "head"), P("seq", "head"))
    return jax.shard_map(shards, mesh=mesh, in_specs=in_specs, out_specs=out_specs, check_vma=False)
```

time: 1790 us -> 557 us (0.31)
  other arithmetic: 662 us -> 4.11 us
  matrix products: 641 us -> 62.8 us
  Pallas kernels: 0 us -> 152 us
  local copies, waits for them, and re-layouts: 104 us -> 6.49 us
  starting transfers between devices: 35.8 us -> 16.5 us
    another operation x3 -> x1, other arithmetic: 634 us -> 0.83 us  [exchange(): return jnp.stack([past_shift, next_source], 1)]
    dot_general x285 -> x16, matrix products: 597 us -> 62.8 us  [the longest x1 16.6 us: shards(): jnp.einsum('td,tc->dc', whole, grad_projected, preferred_element_type=F32)]
    pallas_call x0 -> x2, Pallas kernels: none -> 152 us  [the longest x1 105 us: local_pass(): pl.pallas_call(functools.partial(local_kernel, blocks, unroll), grid=(hea...]
    another operation x3 -> x0, matrix products: 43.5 us -> none  [prepare(): solved = jax.scipy.linalg.solve_triangular(system, targets, lower=True)]
    transpose x6 -> x0, local copies, waits for them, and re-layouts: 27.4 us -> none  [the longest x2 11.4 us: prepare(): jnp.transpose(sections[:, :, 3:5], (1, 0, 2, 3))]
    ppermute x14 -> x6, starting transfers between devices: 35.6 us -> 16.2 us  [shifted(): return lax.ppermute(value.astype(BF), 'seq', pairs).astype(F32)]
    ppermute x14 -> x6, waiting for transfers between devices: 39.2 us -> 21.4 us  [shifted(): return lax.ppermute(value.astype(BF), 'seq', pairs).astype(F32)]
  transfers between devices with their start and end apart: 18 -> 10, of which waited for: 18 -> 8; matrix products, arithmetic and copies ran while one was open for 3% -> 8% of each run, Pallas kernels for 0% -> 0%
where the time goes in v1:
time: 557 us; the launch traced here: 556 us
  waiting for transfers between devices  301 us (54%)
  Pallas kernels  152 us (27%)
  matrix products  62.8 us (11%)
  starting transfers between devices  16.5 us (3%)
  between operations  14 us (3%)
  local copies, waits for them, and re-layouts  6.49 us (1%)
    reduce_scatter x1, waiting for transfers between devices, shards(): lax.psum_scatter(grad_weights.astype(BF), 'seq', scatter_dimension=0, til...  180 us
    pallas_call x1, Pallas kernels, local_pass(): pl.pallas_call(functools.partial(local_kernel, blocks, unroll), grid=(hea...  105 us
    pallas_call x1, Pallas kernels, grad_pass(): pl.pallas_call(functools.partial(grad_kernel, blocks, unroll), grid=(head...  46.4 us
    reduce_scatter x1, waiting for transfers between devices, shards(): lax.psum_scatter(partial_input.astype(BF), 'head', scatter_dimension=1, t...  43.8 us
    all_gather x1, waiting for transfers between devices, shards(): whole = lax.all_gather(layer_input, 'head', axis=1, tiled=True)  38.8 us
    ppermute x6, waiting for transfers between devices, shifted(): return lax.ppermute(value.astype(BF), 'seq', pairs).astype(F32)  21.4 us
    dot_general x1, matrix products, shards(): jnp.einsum('td,tc->dc', whole, grad_projected, preferred_element_type=F32)  16.6 us
    dot_general x1, matrix products, shards(): projected = jnp.dot(whole, w_proj, preferred_element_type=F32).astype(BF)  16.5 us
  transfers between devices with their start and end apart: 10, of which 8 were waited for; matrix products, arithmetic and copies ran while one was open for 8% of the time, Pallas kernels for 0%

profile of v1, /device:TPU:0, one launch (start us, length us, event | category | flops | bytes accessed | tf_op | source)
XLA Modules:
  0.0 556.3 jit_solution(3479301205132083292)
XLA Ops:
  7.2 0.0 copy-start
  7.2 0.0 all-gather.2.cloned.1.call-start
  7.2 0.7 all-gather.2.cloned.1.call-update
  7.9 0.0 reduce-scatter.8.cloned.1.call-start
  8.0 38.8 %all-gather.2.cloned.1.call-done = bf16[1024,2048]{1,0:T(8,128)(2,1)} async-done(((bf16[1024,512]{1,0:T(8,128)(2,1)}), bf16[1024,2048]{1,0:T(8,128)(2,1)}) %all-gather.2.cloned.1.call-update) | async-done | bytes 4194320 | tf_op jit(solution)/shard_map/all_gather | solution.py:449
  46.8 0.0 copy-done
  46.8 3.4 convolution_add_fusion
  50.2 2.0 copy.25
  52.2 16.5 %convolution_convert_fusion.1.proj_ref = bf16[1024,2560]{1,0:T(8,128)(2,1)} fusion(bf16[1024,2048]{1,0:T(8,128)(2,1)} %all-gather.2.cloned.1.call-done, bf16[2048,2560]{1,0:T(8,128)(2,1)} %param.7), kind=kOutput, calls=%fused_computation.3 | convolution fusion | flops 10740039680 | bytes 19922944 | tf_op jit(solution)/shard_map/dot_general | solution.py:452
  68.7 105.4 %local_pass.1 = (bf16[4,16,128,128]{3,2,1,0:T(8,128)(2,1)}, bf16[4,16,128,128]{3,2,1,0:T(8,128)(2,1)}, bf16[4,16,128,128]{3,2,1,0:T(8,128)(2,1)}, bf16[4,16,128,...) custom-call(bf16[128,2048]{1,0:T(8,128)(2,1)} %constant.2.clone.spre, ...), custom_call_target="tpu_custom_call" | custom-call | flops 8053063680 | bytes 33554432 | tf_op jit(solution)/shard_map/local_pass/pallas_call | solution.py:242
  174.1 0.0 copy-start.1
  174.1 1.2 fusion.2
  175.3 0.1 pad_maximum_fusion.2
  175.4 3.4 collective-permute-start
  178.8 1.3 collective-permute-start.3
  180.1 10.3 %collective-permute-done = bf16[4,128,256]{2,1,0:T(8,128)(2,1)S(1)} collective-permute-done((bf16[4,128,256]{2,1,0:T(8,128)(2,1)S(1)}, bf16[4,128,256]{2,1,0:T(8,128)(2,1)S(1)}, u32[]{:S(2)}, u32[]{:S(2)}) %collective-permute-start) | collective-permute-done | bytes 262176 | tf_op jit(solution)/shard_map/ppermute | solution.py:410
  190.4 1.1 add_convert_fusion.6
  191.5 1.1 fusion.18
  192.7 0.0 collective-permute-done.3
  192.7 0.0 copy-done.1
  192.7 0.2 fusion.17
  193.0 3.4 collective-permute-start.1
  196.4 0.2 add_convert_fusion.3
  196.7 1.3 collective-permute-start.4
  198.0 3.8 collective-permute-done.1
  201.8 0.2 add_convert_fusion.5
  202.0 5.3 collective-permute-start.2
  207.3 0.2 fusion.12
  207.5 0.0 collective-permute-done.4
  207.5 0.2 add_convert_fusion.2
  207.8 1.5 collective-permute-start.5
  209.3 0.2 fusion.14
  209.5 0.3 collective-permute-done.2
  209.8 0.3 add_bitcast_fusion.1
  210.1 7.1 %collective-permute-done.5 = bf16[4,128,128]{2,1,0:T(8,128)(2,1)S(1)} collective-permute-done((bf16[4,128,128]{2,1,0:T(8,128)(2,1)S(1)}, bf16[4,128,128]{2,1,0:T(8,128)(2,1)S(1)}, u32[]{:S(2)}, u32[]{:S(2)}) %collective-permute-start.5) | collective-permute-done | bytes 131104 | tf_op jit(solution)/shard_map/ppermute | solution.py:410
  217.2 0.4 add_bitcast_fusion
  217.6 0.8 pad_maximum_fusion.edge_ref
  218.4 46.4 %grad_pass.1 = (bf16[1024,2560]{1,0:T(8,128)(2,1)}, f32[4,1024,2]{2,1,0:T(8,128)}) custom-call(bf16[1024,2560]{1,0:T(8,128)(2,1)} %convolution_convert_fusion.1.proj_ref, f32[4,1024,2]{2,1,0:T(8,128)} %bitcast.58, bf16[1024,512]{1,0:T(8,128)(2,1)} %grad_ref.3, bf16[4,16,128,128]{3,2,1,0:T(8,128)(2,1)} %get-tuple-element.14.key_ref, ...), custom_call_target="tpu_custom_call" | custom-call | flops 4026531840 | bytes 33554432 | tf_op jit(solution)/shard_map/grad_pass/pallas_call | solution.py:368
  264.8 1.7 convert_bitcast_fusion
  266.5 0.4 copy.41
  266.9 3.5 fusion.1
  270.4 0.0 reduce-scatter.8.cloned.1.call-update
  270.4 0.0 reduce-scatter.6.cloned.1.call-start
  270.4 16.6 %fusion = bf16[2048,2560]{0,1:T(8,128)(2,1)} fusion(bf16[1024,2560]{1,0:T(8,128)(2,1)} %get-tuple-element.23, bf16[1024,2048]{1,0:T(8,128)(2,1)} %all-gather.2.cloned.1.call-done), kind=kOutput, calls=%fused_computation.1 | convolution fusion | flops 10742661120 | bytes 19922944 | tf_op jit(solution)/shard_map/td,tc->dc/dot_general | solution.py:465
  287.0 0.0 reduce-scatter.6.cloned.1.call-update
  287.1 0.3 reduce-scatter.4.cloned.1.call-start
  287.3 15.3 %fusion.19 = f32[1024,2048]{1,0:T(8,128)S(1)} fusion(bf16[1024,2560]{1,0:T(8,128)(2,1)} %get-tuple-element.23, bf16[2048,2560]{1,0:T(8,128)(2,1)} %param.7), kind=kOutput, calls=%fused_computation.51 | convolution fusion | flops 10737418240 | bytes 24117248 | tf_op jit(solution)/shard_map/tc,dc->td/dot_general | solution.py:459
  302.7 3.4 add_convert_fusion
  306.0 0.0 reduce-scatter.4.cloned.1.call-update
  306.0 16.0 %reduce-scatter.8.cloned.1.call-done = bf16[256,8]{0,1:T(8,128)(2,1)} async-done(((bf16[2048,8]{0,1:T(8,128)(2,1)}), bf16[256,8]{0,1:T(8,128)(2,1)}) %reduce-scatter.8.cloned.1.call-update) | async-done | bytes 4112 | tf_op jit(solution)/shard_map/reduce_scatter | solution.py:468
  322.0 1.3 convert_element_type.133
  323.3 179.9 %reduce-scatter.6.cloned.1.call-done = bf16[256,2560]{0,1:T(8,128)(2,1)} async-done(((bf16[2048,2560]{0,1:T(8,128)(2,1)}), bf16[256,2560]{0,1:T(8,128)(2,1)}) %reduce-scatter.6.cloned.1.call-update) | async-done | bytes 1310736 | tf_op jit(solution)/shard_map/reduce_scatter | solution.py:467
  503.2 2.8 copy.42
  506.0 43.8 %reduce-scatter.4.cloned.1.call-done = bf16[1024,512]{1,0:T(8,128)(2,1)} async-done(((bf16[1024,2048]{1,0:T(8,128)(2,1)}), bf16[1024,512]{1,0:T(8,128)(2,1)}) %reduce-scatter.4.cloned.1.call-update) | async-done | bytes 1048592 | tf_op jit(solution)/shard_map/reduce_scatter | solution.py:462
  (8 shorter events, 0.3 us)
Async XLA Ops:
  7.2 39.6 %copy-start = (bf16[2048,8]{0,1:T(8,128)(2,1)S(1)}, bf16[2048,8]{0,1:T(8,128)(2,1)}, u32[]{:S(2)}) copy-start(bf16[2048,8]{0,1:T(8,128)(2,1)} %param.8) | copy-start | bytes 98308
  7.2 39.6 %all-gather.2.cloned.1.call-start = ((), (), s32[]{:S(2)}) async-start(), calls=%async_computation.3 | async-start | bytes 5242880 | tf_op jit(solution)/shard_map/all_gather | solution.py:449
  7.9 314.1 %reduce-scatter.8.cloned.1.call-start = ((), (), s32[]{:S(2)}) async-start(), calls=%async_computation.6 | async-start | bytes 36864 | tf_op jit(solution)/shard_map/reduce_scatter | solution.py:468
  174.1 18.7 %copy-start.1 = (f32[4,3,128,128]{3,2,1,0:T(8,128)S(1)}, f32[4,3,128,128]{3,2,1,0:T(8,128)}, u32[]{:S(2)}) copy-start(f32[4,3,128,128]{3,2,1,0:T(8,128)} %get-tuple-element.22) | copy-start | bytes 2359300
  175.4 15.0 %collective-permute-start = (bf16[4,128,256]{2,1,0:T(8,128)(2,1)S(1)}, bf16[4,128,256]{2,1,0:T(8,128)(2,1)S(1)}, u32[]{:S(2)}, u32[]{:S(2)}) collective-permute-start(bf16[4,128,256]{2,1,0:T(8,128)(2,1)S(1)} %get-tuple-element.34), channel_id=1, source_target_pairs={{0,4},{4,8},{8,12},{12,16},{16,20},{20,24},{24,28},{1,5},{5,9},{9,... | collective-permute-start | bytes 786440 | tf_op jit(solution)/shard_map/ppermute | solution.py:410
  178.8 13.9 %collective-permute-start.3 = (bf16[4,128,256]{2,1,0:T(8,128)(2,1)S(1)}, bf16[4,128,256]{2,1,0:T(8,128)(2,1)S(1)}, u32[]{:S(2)}, u32[]{:S(2)}) collective-permute-start(bf16[4,128,256]{2,1,0:T(8,128)(2,1)S(1)} %get-tuple-element.35), channel_id=1, source_target_pairs={{4,0},{8,4},{12,8},{16,12},{20,16},{24,20},{28,24},{5,1},{9,5},{13... | collective-permute-start | bytes 786440 | tf_op jit(solution)/shard_map/ppermute | solution.py:410
  193.0 8.7 %collective-permute-start.1 = (bf16[4,128,256]{2,1,0:T(8,128)(2,1)S(1)}, bf16[4,128,256]{2,1,0:T(8,128)(2,1)S(1)}, u32[]{:S(2)}, u32[]{:S(2)}) collective-permute-start(bf16[4,128,256]{2,1,0:T(8,128)(2,1)S(1)} %pad_maximum_fusion.3), channel_id=1, source_target_pairs={{0,8},{4,12},{8,16},{12,20},{16,24},{20,28},{1,9},{5,13},{9,17},{1... | collective-permute-start | bytes 786440 | tf_op jit(solution)/shard_map/ppermute | solution.py:410
  196.7 10.8 %collective-permute-start.4 = (bf16[4,128,256]{2,1,0:T(8,128)(2,1)S(1)}, bf16[4,128,256]{2,1,0:T(8,128)(2,1)S(1)}, u32[]{:S(2)}, u32[]{:S(2)}) collective-permute-start(bf16[4,128,256]{2,1,0:T(8,128)(2,1)S(1)} %pad_maximum_fusion.4), channel_id=1, source_target_pairs={{8,0},{12,4},{16,8},{20,12},{24,16},{28,20},{9,1},{13,5},{17,9},{2... | collective-permute-start | bytes 786440 | tf_op jit(solution)/shard_map/ppermute | solution.py:410
  202.0 7.8 %collective-permute-start.2 = (bf16[4,128,128]{2,1,0:T(8,128)(2,1)S(1)}, bf16[4,128,128]{2,1,0:T(8,128)(2,1)S(1)}, u32[]{:S(2)}, u32[]{:S(2)}) collective-permute-start(bf16[4,128,128]{2,1,0:T(8,128)(2,1)S(1)} %add_convert_fusion.5), channel_id=1, source_target_pairs={{0,16},{4,20},{8,24},{12,28},{1,17},{5,21},{9,25},{13,29},{2,18},{... | collective-permute-start | bytes 393224 | tf_op jit(solution)/shard_map/ppermute | solution.py:410
  207.8 9.4 %collective-permute-start.5 = (bf16[4,128,128]{2,1,0:T(8,128)(2,1)S(1)}, bf16[4,128,128]{2,1,0:T(8,128)(2,1)S(1)}, u32[]{:S(2)}, u32[]{:S(2)}) collective-permute-start(bf16[4,128,128]{2,1,0:T(8,128)(2,1)S(1)} %add_convert_fusion.2), channel_id=1, source_target_pairs={{16,0},{20,4},{24,8},{28,12},{17,1},{21,5},{25,9},{29,13},{18,2},{... | collective-permute-start | bytes 393224 | tf_op jit(solution)/shard_map/ppermute | solution.py:410
  270.4 232.8 %reduce-scatter.6.cloned.1.call-start = ((), (), s32[]{:S(2)}) async-start(), calls=%async_computation.5 | async-start | bytes 11796480 | tf_op jit(solution)/shard_map/reduce_scatter | solution.py:467
  287.1 262.7 %reduce-scatter.4.cloned.1.call-start = ((), (), s32[]{:S(2)}) async-start(), calls=%async_computation.4 | async-start | bytes 5242880 | tf_op jit(solution)/shard_map/reduce_scatter | solution.py:462
Sparse Core Ops, SparseCore 0:
  9.6 37.1 all-gather.1
  270.5 51.4 reduce-scatter.7
  325.6 177.5 reduce-scatter.5
  506.1 43.5 reduce-scatter.3
